TPU v7x, 512 devices: a whole 4x4x16 slice. The times are simulated.
512 devices in a mesh: bl: 32 (over y, x, core), dir: 16 (over z).
Axes of the slice: x: 4, y: 4, z: 16, core: 2. Of those that a mesh axis runs over, the one named last changes fastest.
Arguments:
- visibilities: float32 [8, 16, 8192], P(None, 'dir', 'bl'), may hold values from -24 to 24
- coherencies: bfloat16 [32, 8, 16, 8192], P('dir', None, None, 'bl'), may hold values from -6 to 6
- gain_offsets: float32 [32, 8, 512], P(None, None, 'bl'), may hold values from -1.5 to 1.5
- stations: int32 [2, 8192], P(None, 'bl'), may hold values from 0 to 511, as said below
- solve_order: int32 [32], replicated, may hold values from 0 to 31, each once
- counts: int32 [32], replicated, may hold values from 1 to 2
- damping: int32 [32], replicated, may hold values from 1 to 8
Outputs:
- gains: float32 [32, 8, 512], P(None, None, 'bl')
- residual: float32 [8, 16, 8192], P(None, 'dir', 'bl')
Inputs may be any that keep to these rules, and one draw needn't show every extreme that they name: Each baseline names two different stations. `solve_order`: each direction appears once.
All inputs are finite; a program needn't handle non-finite values.
Results may differ from a plain program's by a relative error of at most 0.0003.
Values may be sent and summed in bfloat16 or wider, within the bound.
A program may use at most 64 MiB of HBM per device.

v0:
```python
import jax
import jax.numpy as jnp
from jax import lax
from jax.sharding import PartitionSpec as P

LM_ITERS = 2
SOLVED = 4


def matrix_entry(mat, i, j):
    return (mat[4 * i + 2 * j], mat[4 * i + 2 * j + 1])


def matmul_two(left, right):
    pieces = []
    for i in (0, 1):
        for j in (0, 1):
            left_r0, left_i0 = matrix_entry(left, i, 0)
            left_r1, left_i1 = matrix_entry(left, i, 1)
            right_r0, right_i0 = matrix_entry(right, 0, j)
            right_r1, right_i1 = matrix_entry(right, 1, j)
            pieces.append(
                left_r0 * right_r0 - left_i0 * right_i0 + left_r1 * right_r1 - left_i1 * right_i1
            )
            pieces.append(
                left_r0 * right_i0 + left_i0 * right_r0 + left_r1 * right_i1 + left_i1 * right_r1
            )
    return jnp.stack(pieces)


def adjoint(mat):
    return jnp.stack([mat[0], -mat[1], mat[4], -mat[5], mat[2], -mat[3], mat[6], -mat[7]])


def apply_gains(gain_p, coher_now, gain_q):
    return matmul_two(matmul_two(gain_p, coher_now), adjoint(gain_q))


def gram_parts(gram):
    return jnp.stack([gram[0], gram[6], gram[2], gram[3]])


def station_terms(gain_p, gain_q, coher_now, target):
    z_rows = matmul_two(coher_now, adjoint(gain_q))
    y_rows = matmul_two(adjoint(coher_now), adjoint(gain_p))
    leading_endpoint = jnp.concatenate(
        [matmul_two(target, adjoint(z_rows)), gram_parts(matmul_two(z_rows, adjoint(z_rows)))], 0
    )
    second = jnp.concatenate(
        [
            matmul_two(adjoint(target), adjoint(y_rows)),
            gram_parts(matmul_two(y_rows, adjoint(y_rows))),
        ],
        0,
    )
    return (jnp.sum(leading_endpoint, axis=1), jnp.sum(second, axis=1))


def solve_station(gathered_sums, gain_now, damp_value):
    numerator = gathered_sums[:8] + damp_value * gain_now
    diag_a = gathered_sums[8] + damp_value
    diag_d = gathered_sums[9] + damp_value
    cross_r = gathered_sums[10]
    cross_i = gathered_sums[11]
    determinant = diag_a * diag_d - cross_r * cross_r - cross_i * cross_i
    zeros_row = jnp.zeros_like(determinant)
    inverse = (
        jnp.stack([diag_d, zeros_row, -cross_r, -cross_i, -cross_r, cross_i, diag_a, zeros_row])
        / determinant
    )
    return matmul_two(numerator, inverse)


def on_device(visibilities, coherencies, gain_offsets, stations, solve_order, counts, damping):
    identity = jnp.zeros((8,), jnp.float32).at[0].set(1.0).at[6].set(1.0)
    start = lax.all_gather(gain_offsets, "bl", axis=2, tiled=True) + identity[None, :, None]
    groups = lax.axis_size("bl")
    total_channels = coherencies.shape[2]
    station_count = start.shape[2]
    damping_factor = visibilities.shape[2] * groups * total_channels / station_count
    coher_all = lax.all_to_all(coherencies, "dir", 2, 0, tiled=True)
    ends_p = jnp.take(start, stations[0], axis=2)
    ends_q = jnp.take(start, stations[1], axis=2)
    gain_p = jnp.transpose(ends_p, (1, 0, 2))[:, :, None, :]
    gain_q = jnp.transpose(ends_q, (1, 0, 2))[:, :, None, :]
    coher_f32 = jnp.transpose(coher_all, (1, 0, 2, 3)).astype(jnp.float32)
    first_model = jnp.sum(apply_gains(gain_p, coher_f32, gain_q), axis=1)
    first_residual = visibilities - first_model

    def direction_model(gain_now, coher_now):
        gain_p = jnp.take(gain_now, stations[0], axis=1)[:, None, :]
        gain_q = jnp.take(gain_now, stations[1], axis=1)[:, None, :]
        return apply_gains(gain_p, coher_now, gain_q)

    def sweep(step_index, state):
        gain_table, residual = state
        which = solve_order[step_index]
        coher_now = lax.dynamic_index_in_dim(coher_all, which, 0, keepdims=False).astype(
            jnp.float32
        )
        damp_value = damping[which].astype(jnp.float32) * damping_factor
        gain_start = gain_table[which]
        target = residual + direction_model(gain_start, coher_now)

        def iterate(round_index, gain_now):
            gain_p = jnp.take(gain_now, stations[0], axis=1)[:, None, :]
            gain_q = jnp.take(gain_now, stations[1], axis=1)[:, None, :]
            leading_endpoint, second = station_terms(gain_p, gain_q, coher_now, target)
            local_sums = (
                jax.ops.segment_sum(leading_endpoint.T, stations[0], station_count)
                + jax.ops.segment_sum(second.T, stations[1], station_count)
            ).T
            gathered_sums = lax.psum(local_sums, ("bl", "dir"))
            return solve_station(gathered_sums, gain_now, damp_value)

        rounds = jnp.clip(counts[which], 0, LM_ITERS)
        gain_final = lax.fori_loop(0, rounds, iterate, gain_start)
        residual = target - direction_model(gain_final, coher_now)
        return (gain_table.at[which].set(gain_final), residual)

    gain_table, residual = lax.fori_loop(0, SOLVED, sweep, (start, first_residual))
    own_width = station_count // groups
    gains = lax.dynamic_slice_in_dim(gain_table, lax.axis_index("bl") * own_width, own_width, 2)
    return (gains, residual)


def solution(mesh):
    return jax.shard_map(
        on_device,
        mesh=mesh,
        in_specs=(
            P(None, "dir", "bl"),
            P("dir", None, None, "bl"),
            P(None, None, "bl"),
            P(None, "bl"),
            P(),
            P(),
            P(),
        ),
        out_specs=(P(None, None, "bl"), P(None, "dir", "bl")),
        check_vma=False,
    )
```

profile of v0, /device:TPU:1, one launch (start us, length us, event | category | flops | bytes accessed | tf_op | source)
XLA Modules:
  0.0 847.1 jit_solution(9811879134477437065)
XLA Ops:
  0.6 1.6 copy.1122
  2.2 15.7 %all-to-all-start = ((bf16[2,8,16,256]{3,1,0,2:T(8,128)(2,1)}), bf16[2,8,16,256]{3,1,0,2:T(8,128)(2,1)S(1)}, u32[]{:S(2)}, u32[]{:S(2)}) async-start(bf16[2,8,16,256]{3,1,0,2:T(8,128)(2,1)} %copy.1122), calls=%async_computation | async-start | bytes 262144 | tf_op jit(solution)/shard_map/all_to_all | solution.py:81
  18.0 0.8 fusion.135
  18.8 0.9 copy.1120
  19.7 27.2 %all_gather.3 = f32[32,8,512]{0,1,2:T(8,128)S(1)} all-gather(f32[32,8,16]{0,1,2:T(8,128)S(1)} %copy.1120), channel_id=1, replica_groups=mesh['bl'=32,'dir'=16] {'bl'}, dimensions={2}, use_global_device_ids=true | all-gather | bytes 540672 | tf_op jit(solution)/shard_map/all_gather | solution.py:76
  47.1 0.9 copy.1133
  48.0 2.0 gather_fusion.7
  50.0 1.6 copy.1124
  51.6 2.0 gather_fusion.6
  53.6 1.6 copy.1121
  57.4 788.4 %while.42 = (s32[]{:T(128)}, f32[32,8,512]{2,1,0:T(8,128)S(1)}, f32[8,1,256]{2,1,0:T(1,128)S(1)}, s32[32]{0:T(128)S(1)}, s32[32]{0:T(128)S(1)}, /*index=5*/bf16[...) while((s32[]{:T(128)}, f32[32,8,512]{2,1,0:T(8,128)S(1)}, ...), condition=%wide.region_8.12_spmd, body=%wide.region_1.11_spmd.sunk | while | flops 253464 | bytes 1958014 | solution.py:121
  64.8 109.2 %while.43 = (s32[]{:T(128)}, f32[8,512]{1,0:T(8,128)S(1)}, s32[]{:T(128)}, s32[2,256]{1,0:T(2,128)S(1)}, f32[8,1,256]{2,1,0:T(1,128)S(1)}, /*index=5*/f32[8,1,25...) while((s32[]{:T(128)}, f32[8,512]{1,0:T(8,128)S(1)}, ...), condition=%wide.region_7.10_spmd, body=%wide.region_3.9_spmd.sunk | while | flops 160768 | bytes 1263793 | solution.py:117
  67.0 1.5 scatter_custom_fusion.11
  69.0 1.5 scatter_custom_fusion.10
  70.6 103.1 %psum.9 = f32[12,512]{1,0:T(8,128)S(1)} all-reduce(f32[12,512]{1,0:T(8,128)S(1)} %add_bitcast_fusion.2), channel_id=1, replica_groups=mesh['bl'=32,'dir'=16] {'bl','dir'}, use_global_device_ids=true, to_apply=%region_6.8 | all-reduce | flops 6144 | bytes 49152 | tf_op jit(solution)/shard_map/while/body/eval_jaxpr/while/body/psum | solution.py:113
  174.1 0.7 gather_fusion.4
  174.9 0.7 gather_fusion.5
  175.9 0.8 and_reduce_fusion.2
  184.6 212.3 %while.43 = (s32[]{:T(128)}, f32[8,512]{1,0:T(8,128)S(1)}, s32[]{:T(128)}, s32[2,256]{1,0:T(2,128)S(1)}, f32[8,1,256]{2,1,0:T(1,128)S(1)}, /*index=5*/f32[8,1,25...) while((s32[]{:T(128)}, f32[8,512]{1,0:T(8,128)S(1)}, ...), condition=%wide.region_7.10_spmd, body=%wide.region_3.9_spmd.sunk | while | flops 160768 | bytes 1263793 | solution.py:117
  186.8 1.5 scatter_custom_fusion.11
  188.8 1.5 scatter_custom_fusion.10
  190.4 100.7 %psum.9 = f32[12,512]{1,0:T(8,128)S(1)} all-reduce(f32[12,512]{1,0:T(8,128)S(1)} %add_bitcast_fusion.2), channel_id=1, replica_groups=mesh['bl'=32,'dir'=16] {'bl','dir'}, use_global_device_ids=true, to_apply=%region_6.8 | all-reduce | flops 6144 | bytes 49152 | tf_op jit(solution)/shard_map/while/body/eval_jaxpr/while/body/psum | solution.py:113
  293.6 1.5 scatter_custom_fusion.11
  295.5 1.5 scatter_custom_fusion.10
  297.2 99.4 %psum.9 = f32[12,512]{1,0:T(8,128)S(1)} all-reduce(f32[12,512]{1,0:T(8,128)S(1)} %add_bitcast_fusion.2), channel_id=1, replica_groups=mesh['bl'=32,'dir'=16] {'bl','dir'}, use_global_device_ids=true, to_apply=%region_6.8 | all-reduce | flops 6144 | bytes 49152 | tf_op jit(solution)/shard_map/while/body/eval_jaxpr/while/body/psum | solution.py:113
  397.0 0.7 gather_fusion.4
  397.8 0.7 gather_fusion.5
  398.8 0.8 and_reduce_fusion.2
  407.5 212.1 %while.43 = (s32[]{:T(128)}, f32[8,512]{1,0:T(8,128)S(1)}, s32[]{:T(128)}, s32[2,256]{1,0:T(2,128)S(1)}, f32[8,1,256]{2,1,0:T(1,128)S(1)}, /*index=5*/f32[8,1,25...) while((s32[]{:T(128)}, f32[8,512]{1,0:T(8,128)S(1)}, ...), condition=%wide.region_7.10_spmd, body=%wide.region_3.9_spmd.sunk | while | flops 160768 | bytes 1263793 | solution.py:117
  409.7 1.5 scatter_custom_fusion.11
  411.7 1.5 scatter_custom_fusion.10
  413.3 100.4 %psum.9 = f32[12,512]{1,0:T(8,128)S(1)} all-reduce(f32[12,512]{1,0:T(8,128)S(1)} %add_bitcast_fusion.2), channel_id=1, replica_groups=mesh['bl'=32,'dir'=16] {'bl','dir'}, use_global_device_ids=true, to_apply=%region_6.8 | all-reduce | flops 6144 | bytes 49152 | tf_op jit(solution)/shard_map/while/body/eval_jaxpr/while/body/psum | solution.py:113
  516.2 1.5 scatter_custom_fusion.11
  518.1 1.5 scatter_custom_fusion.10
  519.7 99.6 %psum.9 = f32[12,512]{1,0:T(8,128)S(1)} all-reduce(f32[12,512]{1,0:T(8,128)S(1)} %add_bitcast_fusion.2), channel_id=1, replica_groups=mesh['bl'=32,'dir'=16] {'bl','dir'}, use_global_device_ids=true, to_apply=%region_6.8 | all-reduce | flops 6144 | bytes 49152 | tf_op jit(solution)/shard_map/while/body/eval_jaxpr/while/body/psum | solution.py:113
  619.7 0.7 gather_fusion.4
  620.5 0.7 gather_fusion.5
  621.5 0.8 and_reduce_fusion.2
  630.2 212.2 %while.43 = (s32[]{:T(128)}, f32[8,512]{1,0:T(8,128)S(1)}, s32[]{:T(128)}, s32[2,256]{1,0:T(2,128)S(1)}, f32[8,1,256]{2,1,0:T(1,128)S(1)}, /*index=5*/f32[8,1,25...) while((s32[]{:T(128)}, f32[8,512]{1,0:T(8,128)S(1)}, ...), condition=%wide.region_7.10_spmd, body=%wide.region_3.9_spmd.sunk | while | flops 160768 | bytes 1263793 | solution.py:117
  632.5 1.5 scatter_custom_fusion.11
  634.4 1.5 scatter_custom_fusion.10
  636.0 100.5 %psum.9 = f32[12,512]{1,0:T(8,128)S(1)} all-reduce(f32[12,512]{1,0:T(8,128)S(1)} %add_bitcast_fusion.2), channel_id=1, replica_groups=mesh['bl'=32,'dir'=16] {'bl','dir'}, use_global_device_ids=true, to_apply=%region_6.8 | all-reduce | flops 6144 | bytes 49152 | tf_op jit(solution)/shard_map/while/body/eval_jaxpr/while/body/psum | solution.py:113
  739.0 1.5 scatter_custom_fusion.11
  740.9 1.5 scatter_custom_fusion.10
  742.5 99.6 %psum.9 = f32[12,512]{1,0:T(8,128)S(1)} all-reduce(f32[12,512]{1,0:T(8,128)S(1)} %add_bitcast_fusion.2), channel_id=1, replica_groups=mesh['bl'=32,'dir'=16] {'bl','dir'}, use_global_device_ids=true, to_apply=%region_6.8 | all-reduce | flops 6144 | bytes 49152 | tf_op jit(solution)/shard_map/while/body/eval_jaxpr/while/body/psum | solution.py:113
  842.5 0.7 gather_fusion.4
  843.3 0.7 gather_fusion.5
  844.3 0.8 and_reduce_fusion.2
  (579 shorter events, 43.3 us)
Async XLA Ops:
  0.6 46.2 %copy-start.4 = (f32[8]{0:T(128)S(1)}, f32[8]{0:T(128)}, u32[]{:S(2)}) copy-start(f32[8]{0:T(128)} %constant.188.clone.1) | copy-start | bytes 100
  2.2 53.1 %all-to-all-start = ((bf16[2,8,16,256]{3,1,0,2:T(8,128)(2,1)}), bf16[2,8,16,256]{3,1,0,2:T(8,128)(2,1)S(1)}, u32[]{:S(2)}, u32[]{:S(2)}) async-start(bf16[2,8,16,256]{3,1,0,2:T(8,128)(2,1)} %copy.1122), calls=%async_computation | async-start | bytes 262144 | tf_op jit(solution)/shard_map/all_to_all | solution.py:81
  55.2 2.1 copy-start.3
  55.2 2.1 copy-start
  55.3 2.1 copy-start.2
  55.3 2.1 copy-start.5
  55.3 2.1 copy-start.6
  55.3 2.1 copy-start.7
  845.8 1.3 copy-start.1
where the time goes:
time: 849 us; the launch traced here: 847 us
  blocking collectives  731 us (86%)
  local copies, waits for them, and re-layouts  49.5 us (6%)
  other arithmetic  35.1 us (4%)
  starting transfers between devices  15.7 us (2%)
  loops' own time  15.3 us (2%)
    psum x7, blocking collectives, iterate(): gathered_sums = lax.psum(local_sums, ('bl', 'dir'))  703 us
    all_gather x1, blocking collectives, on_device(): lax.all_gather(gain_offsets, 'bl', axis=2, tiled=True)  27.2 us
  transfers between devices with their start and end apart: 1, of which 0 were waited for; matrix products, arithmetic and copies ran while one was open for 1% of the time, Pallas kernels for 0%

commit v1 on v0

--- a/solution.py
+++ b/solution.py
@@ -110,7 +110,7 @@
                 jax.ops.segment_sum(leading_endpoint.T, stations[0], station_count)
                 + jax.ops.segment_sum(second.T, stations[1], station_count)
             ).T
-            gathered_sums = lax.psum(local_sums, ("bl", "dir"))
+            gathered_sums = lax.psum(lax.psum(local_sums, "dir"), "bl")
             return solve_station(gathered_sums, gain_now, damp_value)
 
         rounds = jnp.clip(counts[which], 0, LM_ITERS)

time: 849 us -> 1380 us (1.63)
  blocking collectives: 731 us -> 1260 us
    psum x7 -> x14, blocking collectives: 703 us -> 1240 us  [iterate(): gathered_sums = lax.psum(lax.psum(local_sums, 'dir'), 'bl')]
where the time goes in v1:
time: 1380 us
  blocking collectives  1260 us (91%)
  local copies, waits for them, and re-layouts  49.6 us (4%)
  other arithmetic  34.7 us (3%)
  starting transfers between devices  15.7 us (1%)
  loops' own time  15.3 us (1%)
    psum x14, blocking collectives, iterate(): gathered_sums = lax.psum(lax.psum(local_sums, 'dir'), 'bl')  1240 us
  transfers between devices with their start and end apart: 1, of which 0 were waited for; matrix products, arithmetic and copies ran while one was open for 1% of the time, Pallas kernels for 0%

profile of v1, /device:TPU:1, one launch (start us, length us, event | category | flops | bytes accessed | tf_op | source)
XLA Modules:
  0.0 1379.8 jit_solution(3845699675552759697)
XLA Ops:
  0.6 1.6 copy.1122
  2.3 15.7 %all-to-all-start = ((bf16[2,8,16,256]{3,1,0,2:T(8,128)(2,1)}), bf16[2,8,16,256]{3,1,0,2:T(8,128)(2,1)S(1)}, u32[]{:S(2)}, u32[]{:S(2)}) async-start(bf16[2,8,16,256]{3,1,0,2:T(8,128)(2,1)} %copy.1122), calls=%async_computation | async-start | bytes 262144 | tf_op jit(solution)/shard_map/all_to_all | solution.py:81
  18.0 0.8 fusion.135
  18.8 0.9 copy.1120
  19.7 27.2 %all_gather.3 = f32[32,8,512]{0,1,2:T(8,128)S(1)} all-gather(f32[32,8,16]{0,1,2:T(8,128)S(1)} %copy.1120), channel_id=1, replica_groups=mesh['bl'=32,'dir'=16] {'bl'}, dimensions={2}, use_global_device_ids=true | all-gather | bytes 540672 | tf_op jit(solution)/shard_map/all_gather | solution.py:76
  47.1 0.9 copy.1133
  48.0 2.0 gather_fusion.7
  50.0 1.6 copy.1124
  51.6 2.0 gather_fusion.6
  53.6 1.6 copy.1121
  57.4 1321.1 %while.42 = (s32[]{:T(128)}, f32[32,8,512]{2,1,0:T(8,128)S(1)}, f32[8,1,256]{2,1,0:T(1,128)S(1)}, s32[32]{0:T(128)S(1)}, s32[32]{0:T(128)S(1)}, /*index=5*/bf16[...) while((s32[]{:T(128)}, f32[32,8,512]{2,1,0:T(8,128)S(1)}, ...), condition=%wide.region_9.13_spmd, body=%wide.region_1.12_spmd.sunk | while | flops 259608 | bytes 2007166 | solution.py:121
  64.8 180.6 %while.43 = (s32[]{:T(128)}, f32[8,512]{1,0:T(8,128)S(1)}, s32[]{:T(128)}, s32[2,256]{1,0:T(2,128)S(1)}, f32[8,1,256]{2,1,0:T(1,128)S(1)}, /*index=5*/f32[8,1,25...) while((s32[]{:T(128)}, f32[8,512]{1,0:T(8,128)S(1)}, ...), condition=%wide.region_8.11_spmd, body=%wide.region_3.10_spmd.sunk | while | flops 166912 | bytes 1312945 | solution.py:117
  67.0 1.5 scatter_custom_fusion.11
  69.0 1.5 scatter_custom_fusion.10
  70.6 43.2 %psum.18 = f32[12,512]{1,0:T(8,128)S(1)} all-reduce(f32[12,512]{1,0:T(8,128)S(1)} %add_bitcast_fusion.2), channel_id=1, replica_groups=mesh['bl'=32,'dir'=16] {'dir'}, use_global_device_ids=true, to_apply=%region_6.8 | all-reduce | flops 6144 | bytes 49152 | tf_op jit(solution)/shard_map/while/body/eval_jaxpr/while/body/psum | solution.py:113
  113.8 131.3 %psum.19 = f32[12,512]{1,0:T(8,128)S(1)} all-reduce(f32[12,512]{1,0:T(8,128)S(1)} %psum.18), channel_id=1, replica_groups=mesh['bl'=32,'dir'=16] {'bl'}, use_global_device_ids=true, to_apply=%region_7.9 | all-reduce | flops 6144 | bytes 49152 | tf_op jit(solution)/shard_map/while/body/eval_jaxpr/while/body/psum | solution.py:113
  246.3 0.7 gather_fusion.5
  247.4 0.7 and_reduce_fusion.2
  255.9 366.8 %while.43 = (s32[]{:T(128)}, f32[8,512]{1,0:T(8,128)S(1)}, s32[]{:T(128)}, s32[2,256]{1,0:T(2,128)S(1)}, f32[8,1,256]{2,1,0:T(1,128)S(1)}, /*index=5*/f32[8,1,25...) while((s32[]{:T(128)}, f32[8,512]{1,0:T(8,128)S(1)}, ...), condition=%wide.region_8.11_spmd, body=%wide.region_3.10_spmd.sunk | while | flops 166912 | bytes 1312945 | solution.py:117
  258.2 1.5 scatter_custom_fusion.11
  260.1 1.5 scatter_custom_fusion.10
  261.7 39.7 %psum.18 = f32[12,512]{1,0:T(8,128)S(1)} all-reduce(f32[12,512]{1,0:T(8,128)S(1)} %add_bitcast_fusion.2), channel_id=1, replica_groups=mesh['bl'=32,'dir'=16] {'dir'}, use_global_device_ids=true, to_apply=%region_6.8 | all-reduce | flops 6144 | bytes 49152 | tf_op jit(solution)/shard_map/while/body/eval_jaxpr/while/body/psum | solution.py:113
  301.4 137.7 %psum.19 = f32[12,512]{1,0:T(8,128)S(1)} all-reduce(f32[12,512]{1,0:T(8,128)S(1)} %psum.18), channel_id=1, replica_groups=mesh['bl'=32,'dir'=16] {'bl'}, use_global_device_ids=true, to_apply=%region_7.9 | all-reduce | flops 6144 | bytes 49152 | tf_op jit(solution)/shard_map/while/body/eval_jaxpr/while/body/psum | solution.py:113
  441.6 1.5 scatter_custom_fusion.11
  443.5 1.5 scatter_custom_fusion.10
  445.2 39.6 %psum.18 = f32[12,512]{1,0:T(8,128)S(1)} all-reduce(f32[12,512]{1,0:T(8,128)S(1)} %add_bitcast_fusion.2), channel_id=1, replica_groups=mesh['bl'=32,'dir'=16] {'dir'}, use_global_device_ids=true, to_apply=%region_6.8 | all-reduce | flops 6144 | bytes 49152 | tf_op jit(solution)/shard_map/while/body/eval_jaxpr/while/body/psum | solution.py:113
  484.8 137.7 %psum.19 = f32[12,512]{1,0:T(8,128)S(1)} all-reduce(f32[12,512]{1,0:T(8,128)S(1)} %psum.18), channel_id=1, replica_groups=mesh['bl'=32,'dir'=16] {'bl'}, use_global_device_ids=true, to_apply=%region_7.9 | all-reduce | flops 6144 | bytes 49152 | tf_op jit(solution)/shard_map/while/body/eval_jaxpr/while/body/psum | solution.py:113
  624.7 0.7 and_reduce_fusion.2
  633.3 365.7 %while.43 = (s32[]{:T(128)}, f32[8,512]{1,0:T(8,128)S(1)}, s32[]{:T(128)}, s32[2,256]{1,0:T(2,128)S(1)}, f32[8,1,256]{2,1,0:T(1,128)S(1)}, /*index=5*/f32[8,1,25...) while((s32[]{:T(128)}, f32[8,512]{1,0:T(8,128)S(1)}, ...), condition=%wide.region_8.11_spmd, body=%wide.region_3.10_spmd.sunk | while | flops 166912 | bytes 1312945 | solution.py:117
  635.5 1.5 scatter_custom_fusion.11
  637.5 1.5 scatter_custom_fusion.10
  639.1 39.1 %psum.18 = f32[12,512]{1,0:T(8,128)S(1)} all-reduce(f32[12,512]{1,0:T(8,128)S(1)} %add_bitcast_fusion.2), channel_id=1, replica_groups=mesh['bl'=32,'dir'=16] {'dir'}, use_global_device_ids=true, to_apply=%region_6.8 | all-reduce | flops 6144 | bytes 49152 | tf_op jit(solution)/shard_map/while/body/eval_jaxpr/while/body/psum | solution.py:113
  678.2 137.4 %psum.19 = f32[12,512]{1,0:T(8,128)S(1)} all-reduce(f32[12,512]{1,0:T(8,128)S(1)} %psum.18), channel_id=1, replica_groups=mesh['bl'=32,'dir'=16] {'bl'}, use_global_device_ids=true, to_apply=%region_7.9 | all-reduce | flops 6144 | bytes 49152 | tf_op jit(solution)/shard_map/while/body/eval_jaxpr/while/body/psum | solution.py:113
  818.1 1.5 scatter_custom_fusion.11
  820.0 1.5 scatter_custom_fusion.10
  821.7 39.9 %psum.18 = f32[12,512]{1,0:T(8,128)S(1)} all-reduce(f32[12,512]{1,0:T(8,128)S(1)} %add_bitcast_fusion.2), channel_id=1, replica_groups=mesh['bl'=32,'dir'=16] {'dir'}, use_global_device_ids=true, to_apply=%region_6.8 | all-reduce | flops 6144 | bytes 49152 | tf_op jit(solution)/shard_map/while/body/eval_jaxpr/while/body/psum | solution.py:113
  861.6 137.1 %psum.19 = f32[12,512]{1,0:T(8,128)S(1)} all-reduce(f32[12,512]{1,0:T(8,128)S(1)} %psum.18), channel_id=1, replica_groups=mesh['bl'=32,'dir'=16] {'bl'}, use_global_device_ids=true, to_apply=%region_7.9 | all-reduce | flops 6144 | bytes 49152 | tf_op jit(solution)/shard_map/while/body/eval_jaxpr/while/body/psum | solution.py:113
  1000.9 0.7 and_reduce_fusion.2
  1009.5 365.6 %while.43 = (s32[]{:T(128)}, f32[8,512]{1,0:T(8,128)S(1)}, s32[]{:T(128)}, s32[2,256]{1,0:T(2,128)S(1)}, f32[8,1,256]{2,1,0:T(1,128)S(1)}, /*index=5*/f32[8,1,25...) while((s32[]{:T(128)}, f32[8,512]{1,0:T(8,128)S(1)}, ...), condition=%wide.region_8.11_spmd, body=%wide.region_3.10_spmd.sunk | while | flops 166912 | bytes 1312945 | solution.py:117
  1011.8 1.5 scatter_custom_fusion.11
  1013.7 1.5 scatter_custom_fusion.10
  1015.3 39.1 %psum.18 = f32[12,512]{1,0:T(8,128)S(1)} all-reduce(f32[12,512]{1,0:T(8,128)S(1)} %add_bitcast_fusion.2), channel_id=1, replica_groups=mesh['bl'=32,'dir'=16] {'dir'}, use_global_device_ids=true, to_apply=%region_6.8 | all-reduce | flops 6144 | bytes 49152 | tf_op jit(solution)/shard_map/while/body/eval_jaxpr/while/body/psum | solution.py:113
  1054.4 137.4 %psum.19 = f32[12,512]{1,0:T(8,128)S(1)} all-reduce(f32[12,512]{1,0:T(8,128)S(1)} %psum.18), channel_id=1, replica_groups=mesh['bl'=32,'dir'=16] {'bl'}, use_global_device_ids=true, to_apply=%region_7.9 | all-reduce | flops 6144 | bytes 49152 | tf_op jit(solution)/shard_map/while/body/eval_jaxpr/while/body/psum | solution.py:113
  1194.3 1.5 scatter_custom_fusion.11
  1196.3 1.5 scatter_custom_fusion.10
  1197.9 39.6 %psum.18 = f32[12,512]{1,0:T(8,128)S(1)} all-reduce(f32[12,512]{1,0:T(8,128)S(1)} %add_bitcast_fusion.2), channel_id=1, replica_groups=mesh['bl'=32,'dir'=16] {'dir'}, use_global_device_ids=true, to_apply=%region_6.8 | all-reduce | flops 6144 | bytes 49152 | tf_op jit(solution)/shard_map/while/body/eval_jaxpr/while/body/psum | solution.py:113
  1237.5 137.4 %psum.19 = f32[12,512]{1,0:T(8,128)S(1)} all-reduce(f32[12,512]{1,0:T(8,128)S(1)} %psum.18), channel_id=1, replica_groups=mesh['bl'=32,'dir'=16] {'bl'}, use_global_device_ids=true, to_apply=%region_7.9 | all-reduce | flops 6144 | bytes 49152 | tf_op jit(solution)/shard_map/while/body/eval_jaxpr/while/body/psum | solution.py:113
  1377.1 0.7 and_reduce_fusion.2
  (586 shorter events, 48.3 us)
Async XLA Ops:
  0.6 46.2 %copy-start.4 = (f32[8]{0:T(128)S(1)}, f32[8]{0:T(128)}, u32[]{:S(2)}) copy-start(f32[8]{0:T(128)} %constant.188.clone.1) | copy-start | bytes 100
  2.3 53.1 %all-to-all-start = ((bf16[2,8,16,256]{3,1,0,2:T(8,128)(2,1)}), bf16[2,8,16,256]{3,1,0,2:T(8,128)(2,1)S(1)}, u32[]{:S(2)}, u32[]{:S(2)}) async-start(bf16[2,8,16,256]{3,1,0,2:T(8,128)(2,1)} %copy.1122), calls=%async_computation | async-start | bytes 262144 | tf_op jit(solution)/shard_map/all_to_all | solution.py:81
  55.2 2.1 copy-start.3
  55.2 2.1 copy-start
  55.3 2.1 copy-start.2
  55.3 2.1 copy-start.5
  55.3 2.1 copy-start.6
  55.3 2.1 copy-start.7
  1378.5 1.3 copy-start.1
